TPU v7x, 32 devices: a whole 2x2x4 slice. The times are simulated.
32 devices in a mesh: rows: 16 (over z, y, x), cols: 2 (over core).
Axes of the slice: x: 2, y: 2, z: 4, core: 2. Of those that a mesh axis runs over, the one named last changes fastest.
Arguments:
- grad: float32 [6144, 16384], P('rows', 'cols'), may hold values from -200 to 200
- projection: float32 [512, 6144], P(None, 'rows'), may hold values from -1.5 to 1.5
- moment1: float32 [512, 16384], P('rows', 'cols'), may hold values from -6 to 6
- moment2: float32 [512, 16384], P('rows', 'cols'), may hold values from 0.05 to 3
Outputs:
- update: float32 [6144, 16384], P('rows', 'cols')
- moment1_new: float32 [512, 16384], P('rows', 'cols')
- moment2_new: float32 [512, 16384], P('rows', 'cols')
All inputs are finite; a program needn't handle non-finite values.
Results may differ from a plain program's by a relative error of at most 0.00007.
Values sent between devices are 32-bit elements; how exact they have to be, the bound alone decides.
A program may use at most 128 MiB of HBM per device.

v0:
```python
import jax
import jax.numpy as jnp
from jax import lax
from jax.sharding import PartitionSpec as P

D = 6144
FF = 16384
RANK = 512
STEP = 100


def shards(grad, projection, moment1, moment2):
    total = lax.psum(jnp.sum(grad * grad), ("rows", "cols"))
    clip = jnp.minimum(1.0, 0.5 / jnp.sqrt(total / (D * FF) + 1e-06))
    proj = (
        lax.psum_scatter(
            jnp.dot(
                projection,
                grad,
                precision=lax.Precision.HIGHEST,
                preferred_element_type=jnp.float32,
            ),
            "rows",
            scatter_dimension=0,
            tiled=True,
        )
        * clip
    )
    moment1_new = 0.9 * moment1 + 0.1 * proj
    moment2_new = 0.999 * moment2 + 0.001 * proj * proj
    first_fix = 1.0 - 0.9**STEP
    second_fix = 1.0 - 0.999**STEP
    adapted = moment1_new / first_fix / (jnp.sqrt(moment2_new / second_fix) + 1e-08)
    part_adapted = jnp.sum(adapted * adapted, axis=0)
    part_proj = jnp.sum(proj * proj, axis=0)
    col_adapted, col_proj = lax.psum((part_adapted, part_proj), "rows")
    scale = jnp.sqrt(col_adapted / RANK + 1e-06) / jnp.sqrt(col_proj / RANK + 1e-06)
    update = grad * (clip * scale)[None, :]
    return (update, moment1_new, moment2_new)


def solution(mesh):
    return jax.shard_map(
        shards,
        mesh=mesh,
        in_specs=(P("rows", "cols"), P(None, "rows"), P("rows", "cols"), P("rows", "cols")),
        out_specs=(P("rows", "cols"), P("rows", "cols"), P("rows", "cols")),
        check_vma=False,
    )
```

profile of v0, /device:TPU:0, one launch (start us, length us, event | category | flops | bytes accessed | tf_op | source)
XLA Modules:
  0.0 524.4 jit_solution(5903958585262817812)
XLA Ops:
  7.2 0.0 copy-start
  7.2 0.0 reduce-scatter.2.cloned.1.call-start
  7.2 1.1 copy-done
  8.3 30.8 %fusion.2 = f32[512,8192]{1,0:T(8,128)} fusion(f32[512,384]{1,0:T(8,128)S(1)} %copy-done, f32[384,8192]{1,0:T(8,128)} %param.4), kind=kOutput, calls=%fused_computation.8 | convolution fusion | flops 19327352832 | bytes 30146560 | tf_op jit(solution)/shard_map/dot_general | solution.py:17
  39.1 0.0 copy-start.1
  39.1 0.0 copy-start.2
  39.1 0.0 reduce-scatter.2.cloned.1.call-update
  39.1 0.0 all-reduce.3.cloned.1.call-start
  39.2 8.6 %multiply_reduce_fusion = f32[]{:T(128)} fusion(f32[384,8192]{1,0:T(8,128)} %param.4), kind=kLoop, calls=%fused_computation | loop fusion | flops 6291455 | bytes 12582916 | tf_op jit(solution)/shard_map/reduce_sum | solution.py:13
  47.7 62.6 %psum.21 = f32[]{:T(128)} all-reduce(f32[]{:T(128)} %multiply_reduce_fusion), channel_id=1, replica_groups=mesh['rows'=16,'cols'=2] {'rows','cols'}, use_global_device_ids=true, to_apply=%region_1.0 | all-reduce | flops 1 | bytes 8 | tf_op jit(solution)/shard_map/psum | solution.py:13
  111.0 278.8 %reduce-scatter.2.cloned.1.call-done = f32[32,8192]{1,0:T(8,128)} async-done(((f32[512,8192]{1,0:T(8,128)}), f32[32,8192]{1,0:T(8,128)}) %reduce-scatter.2.cloned.1.call-update) | async-done | bytes 1048592 | tf_op jit(solution)/shard_map/reduce_scatter | solution.py:16
  389.8 0.0 copy-done.1
  389.9 0.0 copy-done.2
  389.9 4.1 multiply_reduce_fusion.2
  393.9 0.0 all-reduce.3.cloned.1.call-update
  393.9 111.5 %all-reduce.3.cloned.1.call-done = (f32[8192]{0:T(1024)}, f32[8192]{0:T(1024)}) async-done(((f32[8192]{0:T(1024)}, f32[8192]{0:T(1024)}), (f32[8192]{0:T(1024)}, f32[8192]{0:T(1024)})) %all-reduce.3.cloned.1.call-update) | async-done | bytes 65552 | tf_op jit(solution)/shard_map/psum | solution.py:36
  505.5 0.8 multiply_multiply_fusion.1
  506.3 11.3 %broadcast_multiply_fusion = f32[384,8192]{1,0:T(8,128)} fusion(f32[384,8192]{1,0:T(8,128)} %param.4, f32[8192]{0:T(1024)S(1)} %multiply_multiply_fusion.1), kind=kLoop, calls=%fused_computation.1 | loop fusion | flops 3145728 | bytes 25198592 | tf_op jit(solution)/shard_map/mul | solution.py:38
Async XLA Ops:
  7.2 1.1 copy-start
  7.2 382.7 %reduce-scatter.2.cloned.1.call-start = ((), (), s32[]{:S(2)}) async-start(), calls=%async_computation.1 | async-start | bytes 17825792 | tf_op jit(solution)/shard_map/reduce_scatter | solution.py:16
  39.1 350.7 %copy-start.1 = (f32[32,8192]{1,0:T(8,128)S(1)}, f32[32,8192]{1,0:T(8,128)}, u32[]{:S(2)}) copy-start(f32[32,8192]{1,0:T(8,128)} %param.6) | copy-start | bytes 3145732
  39.1 350.7 %copy-start.2 = (f32[32,8192]{1,0:T(8,128)S(1)}, f32[32,8192]{1,0:T(8,128)}, u32[]{:S(2)}) copy-start(f32[32,8192]{1,0:T(8,128)} %param.7) | copy-start | bytes 3145732
  39.1 466.3 %all-reduce.3.cloned.1.call-start = ((), (), s32[]{:S(2)}) async-start(), calls=%async_computation.2 | async-start | bytes 131072 | tf_op jit(solution)/shard_map/psum | solution.py:36
Sparse Core Ops, SparseCore 0:
  39.3 350.5 reduce-scatter.1
  396.0 109.4 all-reduce.2
where the time goes:
time: 525 us; the launch traced here: 524 us
  waiting for transfers between devices  390 us (74%)
  blocking collectives  62.6 us (12%)
  matrix products  30.8 us (6%)
  other arithmetic  24.7 us (5%)
  between operations  14.7 us (3%)
    reduce_scatter x1, waiting for transfers between devices, shards(): lax.psum_scatter(jnp.dot(projection, grad, precision=lax.Precision.HIGHES...  279 us
    psum x1, waiting for transfers between devices, shards(): col_adapted, col_proj = lax.psum((part_adapted, part_proj), 'rows')  112 us
    psum x1, blocking collectives, shards(): total = lax.psum(jnp.sum(grad * grad), ('rows', 'cols'))  62.6 us
    dot_general x1, matrix products, shards(): jnp.dot(projection, grad, precision=lax.Precision.HIGHEST, preferred_elem...  30.8 us
    mul x2, other arithmetic, shards(): update = grad * (clip * scale)[None, :]  12.1 us
  transfers between devices with their start and end apart: 2, of which 2 were waited for; matrix products, arithmetic and copies ran while one was open for 2% of the time, Pallas kernels for 0%

commit v1 on v0

v1 whole, which is shorter than its diff:
```python
import functools

import jax
import jax.numpy as jnp
from jax import lax
from jax.experimental import pallas as pl
from jax.experimental.pallas import tpu as pltpu
from jax.sharding import PartitionSpec as P

D = 6144
FF = 16384
RANK = 512
STEP = 100
MESH = pl.DeviceIdType.MESH


def kernel(cfg, grad, projection, m1, m2, m1o, m2o, fac, gbuf, pp, part, sq, sqr, col, colr, *rest):
    rows_bits, cols_bits, steps, width, orders, lags, ahead = cfg
    stages = rows_bits
    recv = rest[:stages]
    gsem, psem, ssem, rsem, qssem, qrsem, cssem, crsem = rest[stages:]
    n = 1 << rows_bits
    own = RANK // n
    me = lax.axis_index("rows")
    my_col = lax.axis_index("cols")

    def bit_of(index, bit):
        return lax.rem(lax.div(index, 1 << bit), 2)

    def partner(index, bit):
        return index + (1 - 2 * bit_of(index, bit)) * (1 << bit)

    row_bits = [bit_of(me, b) for b in range(rows_bits)]
    row_partner = [{"rows": partner(me, b)} for b in range(rows_bits)]
    col_partner = [{"cols": partner(my_col, b)} for b in range(cols_bits)]

    def load_grad(t):
        return pltpu.make_async_copy(
            grad.at[:, pl.ds(pl.multiple_of(t * (2 * width), 128), 2 * width)],
            gbuf.at[t],
            gsem.at[t],
        )

    def load_projection(lane, block):
        place = sum(((block >> b) & 1) << (stages - 1 - k) for k, b in enumerate(orders[lane]))
        return pltpu.make_async_copy(
            projection.at[pl.ds(block * own, own)],
            pp.at[lane, pl.ds(place * own, own)],
            psem.at[lane, block],
        )

    load_grad(0).start()
    for lane in range(2):
        for block in range(n):
            load_projection(lane, block).start()

    @pl.loop(1, steps)
    def _(t):
        load_grad(t).start()

    barrier = pltpu.get_barrier_semaphore()
    for to in row_partner + col_partner:
        pl.semaphore_signal(barrier, inc=1, device_id=to, device_id_type=MESH)
    pl.semaphore_wait(barrier, rows_bits + cols_bits)

    kept, sent = [], []
    for lane in range(2):
        at, keeps, sends = 0, [0], []
        for k, b in enumerate(orders[lane]):
            half = RANK >> (k + 1)
            sends.append(pl.multiple_of(at + (1 - row_bits[b]) * half, own))
            at = pl.multiple_of(at + row_bits[b] * half, own)
            keeps.append(at)
        kept.append(keeps)
        sent.append(sends)

    def exchange(t, lane, k):
        half = RANK >> (k + 1)
        return pltpu.make_async_remote_copy(
            src_ref=part.at[t, lane, pl.ds(sent[lane][k], half)],
            dst_ref=recv[k].at[t, lane],
            send_sem=ssem.at[t, lane, k],
            recv_sem=rsem.at[t, lane, k],
            device_id=row_partner[orders[lane][k]],
            device_id_type=MESH,
        )

    def multiply(t):
        for lane in range(2):
            part[t, lane] = jnp.dot(
                pp[lane],
                gbuf[t, :, lane * width : (lane + 1) * width],
                precision=lax.Precision.HIGHEST,
                preferred_element_type=jnp.float32,
            )
            exchange(t, lane, 0).start()

    for lane in range(2):
        for block in range(n):
            load_projection(lane, block).wait()

    @pl.loop(0, ahead)
    def _(t):
        load_grad(t).wait()
        multiply(t)

    def squares(t, total):
        g = gbuf[t]
        g = g.reshape(g.shape[0] // 8, 8, g.shape[1])
        return total + jnp.sum(g * g, axis=0)

    def squares_late(t, total):
        load_grad(t).wait()
        return squares(t, total)

    total = jnp.zeros((8, 2 * width), jnp.float32)
    total = lax.fori_loop(0, ahead, squares, total)
    total = lax.fori_loop(ahead, steps, squares_late, total)
    sq[0] = jnp.zeros((8, width), jnp.float32) + jnp.sum(total)
    for j, to in enumerate(row_partner + col_partner):
        copy = pltpu.make_async_remote_copy(
            src_ref=sq.at[j],
            dst_ref=sqr.at[j],
            send_sem=qssem.at[j],
            recv_sem=qrsem.at[j],
            device_id=to,
            device_id_type=MESH,
        )
        copy.start()
        copy.wait()
        sq[j + 1] = sq[j] + sqr[j]
    last = rows_bits + cols_bits
    first_fix = 1.0 - 0.9**STEP
    second_fix = 1.0 - 0.999**STEP

    def clip_row():
        return jnp.minimum(1.0, 0.5 / jnp.sqrt(sq[last, 0:1, :] / (D * FF) + 1e-06))

    def finish(t, k):
        for lane in range(2):
            exchange(t, lane, k).wait_recv()
            mine = pl.ds(kept[lane][k + 1], RANK >> (k + 1))
            if k + 1 < stages:
                part[t, lane, mine] = part[t, lane, mine] + recv[k][t, lane]
                exchange(t, lane, k + 1).start()
            else:
                proj = (part[t, lane, mine] + recv[k][t, lane]) * clip_row()
                cols = pl.ds(pl.multiple_of(t * (2 * width) + lane * width, 128), width)
                first = 0.9 * m1[:, cols] + 0.1 * proj
                second = 0.999 * m2[:, cols] + 0.001 * proj * proj
                m1o[:, cols] = first
                m2o[:, cols] = second
                adapted = first / first_fix / (jnp.sqrt(second / second_fix) + 1e-08)
                col[0, 0:1, cols] = jnp.sum(adapted * adapted, axis=0, keepdims=True)
                col[0, 1:2, cols] = jnp.sum(proj * proj, axis=0, keepdims=True)

    @pl.loop(ahead, steps + lags[-1])
    def _(t):
        @pl.when(t < steps)
        def _():
            multiply(t)

        for k in range(stages):

            @pl.when((t >= lags[k]) & (t < steps + lags[k]))
            def _():
                finish(t - lags[k], k)

    for j, to in enumerate(row_partner):
        copy = pltpu.make_async_remote_copy(
            src_ref=col.at[j],
            dst_ref=colr.at[j],
            send_sem=cssem.at[j],
            recv_sem=crsem.at[j],
            device_id=to,
            device_id_type=MESH,
        )
        copy.start()
        copy.wait()
        col[j + 1] = col[j] + colr[j]
    clip = jnp.minimum(1.0, 0.5 / jnp.sqrt(sq[last, 0:1, 0:1] / (D * FF) + 1e-06))
    both = col[stages]
    scale = jnp.sqrt(both[0:1] / RANK + 1e-06) / jnp.sqrt(both[1:2] / RANK + 1e-06)
    fac[...] = clip * scale

    @pl.loop(0, steps)
    def _(t):
        for lane in range(2):
            for k in range(stages):
                exchange(t, lane, k).wait_send()


def shards(rows, cols, grad, projection, moment1, moment2):
    depth, span = grad.shape
    rows_bits, cols_bits = rows.bit_length() - 1, cols.bit_length() - 1
    width = 256 if span % 512 == 0 else 128
    steps = span // (2 * width)
    own = RANK // rows
    natural = tuple(range(rows_bits))
    orders = (natural, natural[1::-1] + natural[2:])
    ahead = min(3, steps)
    lags = tuple((ahead, ahead + 2)[min(k, 1)] + max(k - 1, 0) for k in range(rows_bits))
    cfg = (rows_bits, cols_bits, steps, width, orders, lags, ahead)
    last = rows_bits + cols_bits
    f32 = jnp.float32
    vmem = pl.BlockSpec(memory_space=pltpu.VMEM)
    hbm = pl.BlockSpec(memory_space=pl.ANY)
    dma = pltpu.SemaphoreType.DMA
    moment1_new, moment2_new, factor = pl.pallas_call(
        functools.partial(kernel, cfg),
        out_shape=(
            jax.ShapeDtypeStruct((own, span), f32),
            jax.ShapeDtypeStruct((own, span), f32),
            jax.ShapeDtypeStruct((1, span), f32),
        ),
        in_specs=[hbm, hbm, vmem, vmem],
        out_specs=[vmem, vmem, vmem],
        scratch_shapes=[
            pltpu.VMEM((steps, depth, 2 * width), f32),
            pltpu.VMEM((2, RANK, depth), f32),
            pltpu.VMEM((steps, 2, RANK, width), f32),
            pltpu.VMEM((last + 1, 8, width), f32),
            pltpu.VMEM((last, 8, width), f32),
            pltpu.VMEM((rows_bits + 1, 2, span), f32),
            pltpu.VMEM((rows_bits, 2, span), f32),
        ]
        + [pltpu.VMEM((steps, 2, RANK >> (k + 1), width), f32) for k in range(rows_bits)]
        + [
            dma((steps,)),
            dma((2, rows)),
            dma((steps, 2, rows_bits)),
            dma((steps, 2, rows_bits)),
            dma((last,)),
            dma((last,)),
            dma((rows_bits,)),
            dma((rows_bits,)),
        ],
        compiler_params=pltpu.CompilerParams(
            collective_id=0, has_side_effects=True, vmem_limit_bytes=67000000
        ),
        name="project_reduce",
    )(grad, projection, moment1, moment2)
    return (grad * factor, moment1_new, moment2_new)


def solution(mesh):
    rows, cols = mesh.shape["rows"], mesh.shape["cols"]
    return jax.shard_map(
        functools.partial(shards, rows, cols),
        mesh=mesh,
        in_specs=(P("rows", "cols"), P(None, "rows"), P("rows", "cols"), P("rows", "cols")),
        out_specs=(P("rows", "cols"), P("rows", "cols"), P("rows", "cols")),
        check_vma=False,
    )
```

time: 525 us -> 208 us (0.40)
  waiting for transfers between devices: 390 us -> 0 us
  Pallas kernels: 0 us -> 194 us
  blocking collectives: 62.6 us -> 0 us
  matrix products: 30.8 us -> 0 us
  between operations: 14.7 us -> 0.66 us
  other arithmetic: 24.7 us -> 11.5 us
    reduce_scatter x1 -> x0, waiting for transfers between devices: 279 us -> none  [shards(): lax.psum_scatter(jnp.dot(projection, grad, precision=lax.Precision.HIGHES...]
    pallas_call x0 -> x1, Pallas kernels: none -> 194 us  [shards(): pl.pallas_call(functools.partial(kernel, cfg), out_shape=(jax.ShapeDtypeS...]
    psum x1 -> x0, waiting for transfers between devices: 112 us -> none  [shards(): col_adapted, col_proj = lax.psum((part_adapted, part_proj), 'rows')]
    psum x1 -> x0, blocking collectives: 62.6 us -> none  [shards(): total = lax.psum(jnp.sum(grad * grad), ('rows', 'cols'))]
    dot_general x1 -> x0, matrix products: 30.8 us -> none  [shards(): jnp.dot(projection, grad, precision=lax.Precision.HIGHEST, preferred_elem...]
    reduce_sum x2 -> x0, other arithmetic: 12.6 us -> none  [the longest x1 8.55 us: shards(): total = lax.psum(jnp.sum(grad * grad), ('rows', 'cols'))]
    mul x2 -> x1, other arithmetic: 12.1 us -> 11.5 us  [shards(): return (grad * factor, moment1_new, moment2_new)]
  transfers between devices with their start and end apart: 2 -> 0, of which waited for: 2 -> 0; matrix products, arithmetic and copies ran while one was open for 2% -> 0% of each run, Pallas kernels for 0% -> 0%
where the time goes in v1:
time: 208 us
  Pallas kernels  194 us (93%)
  other arithmetic  11.5 us (6%)
    pallas_call x1, Pallas kernels, shards(): pl.pallas_call(functools.partial(kernel, cfg), out_shape=(jax.ShapeDtypeS...  194 us
    mul x1, other arithmetic, shards(): return (grad * factor, moment1_new, moment2_new)  11.5 us

profile of v1, /device:TPU:0, one launch (start us, length us, event | category | flops | bytes accessed | tf_op | source)
XLA Modules:
  0.0 207.7 jit_solution(13393682429794982603)
XLA Ops:
  0.6 193.7 %project_reduce.1 = (f32[32,8192]{1,0:T(8,128)}, f32[32,8192]{1,0:T(8,128)}, f32[1,8192]{1,0:T(1,128)}) custom-call(f32[384,8192]{1,0:T(8,128)} %grad.1, f32[512,384]{1,0:T(8,128)} %projection.1, f32[32,8192]{1,0:T(8,128)} %m1.1, f32[32,8192]{1,0:T(8,128)} %m2.1), custom_call_target="tpu_custom_call" | custom-call | tf_op jit(solution)/shard_map/project_reduce/pallas_call | solution.py:209
  194.3 0.0 copy-start.1
  194.3 0.0 copy-start
  194.3 11.5 %broadcast_multiply_fusion = f32[384,8192]{1,0:T(8,128)} fusion(f32[384,8192]{1,0:T(8,128)} %grad.1, f32[8192]{0:T(1024)} %bitcast.1), kind=kLoop, calls=%fused_computation | loop fusion | flops 3145728 | bytes 25198592 | tf_op jit(solution)/shard_map/mul | solution.py:243
  205.8 0.0 copy-done.1
  205.8 1.0 copy.9
  206.7 0.0 copy-done
  206.8 1.0 copy.10
Async XLA Ops:
  194.3 11.5 %copy-start.1 = (f32[32,8192]{1,0:T(8,128)S(1)}, f32[32,8192]{1,0:T(8,128)}, u32[]{:S(2)}) copy-start(f32[32,8192]{1,0:T(8,128)} %get-tuple-element.13) | copy-start | bytes 3145732
  194.3 12.4 %copy-start = (f32[32,8192]{1,0:T(8,128)S(1)}, f32[32,8192]{1,0:T(8,128)}, u32[]{:S(2)}) copy-start(f32[32,8192]{1,0:T(8,128)} %get-tuple-element.14) | copy-start | bytes 3145732

commit v2 on v1

v2 whole, which is shorter than its diff:
```python
import functools

import jax
import jax.numpy as jnp
from jax import lax
from jax.experimental import pallas as pl
from jax.experimental.pallas import tpu as pltpu
from jax.sharding import PartitionSpec as P

D = 6144
FF = 16384
RANK = 512
STEP = 100
MESH = pl.DeviceIdType.MESH


def kernel(cfg, grad, projection, m1, m2, m1o, m2o, fac, gbuf, pp, sq, sqr, col, colr, *rest):
    rows_bits, cols_bits, steps, width, orders, plan, lags, ahead = cfg
    stages = rows_bits
    turns = len(plan)
    lanes = [(u, i) for u in range(turns) for i in range(len(plan[u]))]
    bufs = {lane: rest[at * (stages + 1) : (at + 1) * (stages + 1)] for at, lane in enumerate(lanes)}
    number = {lane: at for at, lane in enumerate(lanes)}
    gsem, psem, ssem, rsem, qssem, qrsem, cssem, crsem = rest[len(lanes) * (stages + 1) :]
    n = 1 << rows_bits
    own = RANK // n
    me = lax.axis_index("rows")
    my_col = lax.axis_index("cols")

    def bit_of(index, bit):
        return lax.rem(lax.div(index, 1 << bit), 2)

    def partner(index, bit):
        return index + (1 - 2 * bit_of(index, bit)) * (1 << bit)

    row_bits = [bit_of(me, b) for b in range(rows_bits)]
    row_partner = [{"rows": partner(me, b)} for b in range(rows_bits)]
    col_partner = [{"cols": partner(my_col, b)} for b in range(cols_bits)]

    def load_grad(t):
        return pltpu.make_async_copy(
            grad.at[:, pl.ds(pl.multiple_of(t * width, 128), width)],
            gbuf.at[t],
            gsem.at[t],
        )

    def load_projection(lane, block):
        place = sum(((block >> b) & 1) << (stages - 1 - k) for k, b in enumerate(orders[lane]))
        return pltpu.make_async_copy(
            projection.at[pl.ds(block * own, own)],
            pp.at[lane, pl.ds(place * own, own)],
            psem.at[lane, block],
        )

    load_grad(0).start()
    for lane in range(len(orders)):
        for block in range(n):
            load_projection(lane, block).start()

    @pl.loop(1, steps)
    def _(t):
        load_grad(t).start()

    barrier = pltpu.get_barrier_semaphore()
    for to in row_partner + col_partner:
        pl.semaphore_signal(barrier, inc=1, device_id=to, device_id_type=MESH)
    pl.semaphore_wait(barrier, rows_bits + cols_bits)

    kept, sent = [], []
    for lane in range(len(orders)):
        at, keeps, sends = 0, [0], []
        for k, b in enumerate(orders[lane]):
            half = RANK >> (k + 1)
            sends.append(pl.multiple_of(at + (1 - row_bits[b]) * half, own))
            at = pl.multiple_of(at + row_bits[b] * half, own)
            keeps.append(at)
        kept.append(keeps)
        sent.append(sends)

    def exchange(p, lane, k):
        kind = plan[lane[0]][lane[1]][0]
        half = RANK >> (k + 1)
        return pltpu.make_async_remote_copy(
            src_ref=bufs[lane][0].at[p, pl.ds(sent[kind][k], half)],
            dst_ref=bufs[lane][k + 1].at[p],
            send_sem=ssem.at[number[lane], p, k],
            recv_sem=rsem.at[number[lane], p, k],
            device_id=row_partner[orders[kind][k]],
            device_id_type=MESH,
        )

    def multiply(p, u):
        for i, (kind, at, wide) in enumerate(plan[u]):
            bufs[u, i][0][p] = jnp.dot(
                pp[kind],
                gbuf[p * turns + u, :, at : at + wide],
                precision=lax.Precision.HIGHEST,
                preferred_element_type=jnp.float32,
            )
            exchange(p, (u, i), 0).start()

    for lane in range(len(orders)):
        for block in range(n):
            load_projection(lane, block).wait()

    for t in range(ahead):
        load_grad(t).wait()
        multiply(t // turns, t % turns)

    def squares(t, total):
        g = gbuf[t]
        g = g.reshape(g.shape[0] // 8, 8, g.shape[1])
        return total + jnp.sum(g * g, axis=0)

    def squares_late(t, total):
        load_grad(t).wait()
        return squares(t, total)

    total = jnp.zeros((8, width), jnp.float32)
    total = lax.fori_loop(0, ahead, squares, total)
    total = lax.fori_loop(ahead, steps, squares_late, total)
    sq[0] = jnp.zeros(sq.shape[1:], jnp.float32) + jnp.sum(total)
    for j, to in enumerate(row_partner + col_partner):
        copy = pltpu.make_async_remote_copy(
            src_ref=sq.at[j],
            dst_ref=sqr.at[j],
            send_sem=qssem.at[j],
            recv_sem=qrsem.at[j],
            device_id=to,
            device_id_type=MESH,
        )
        copy.start()
        copy.wait()
        sq[j + 1] = sq[j] + sqr[j]
    last = rows_bits + cols_bits
    first_fix = 1.0 - 0.9**STEP
    second_fix = 1.0 - 0.999**STEP

    def clip_row(wide):
        return jnp.minimum(1.0, 0.5 / jnp.sqrt(sq[last, 0:1, :wide] / (D * FF) + 1e-06))

    def finish(p, u, k):
        for i, (kind, at, wide) in enumerate(plan[u]):
            part, recv = bufs[u, i][0], bufs[u, i][k + 1]
            exchange(p, (u, i), k).wait_recv()
            mine = pl.ds(kept[kind][k + 1], RANK >> (k + 1))
            if k + 1 < stages:
                part[p, mine] = part[p, mine] + recv[p]
                exchange(p, (u, i), k + 1).start()
            else:
                proj = (part[p, mine] + recv[p]) * clip_row(wide)
                cols = pl.ds(pl.multiple_of((p * turns + u) * width + at, 128), wide)
                first = 0.9 * m1[:, cols] + 0.1 * proj
                second = 0.999 * m2[:, cols] + 0.001 * proj * proj
                m1o[:, cols] = first
                m2o[:, cols] = second
                adapted = first / first_fix / (jnp.sqrt(second / second_fix) + 1e-08)
                h = lax.div(p, steps // turns // 2)
                cols = pl.ds(pl.multiple_of((p * turns + u) * width + at - h * col.shape[-1], 128), wide)
                col[0, h, 0:1, cols] = jnp.sum(adapted * adapted, axis=0, keepdims=True)
                col[0, h, 1:2, cols] = jnp.sum(proj * proj, axis=0, keepdims=True)

    @pl.loop(ahead // turns, -(-(steps + lags[-1]) // turns))
    def _(p):
        for u in range(turns):

            @pl.when(p * turns + u < steps)
            def _():
                multiply(p, u)

            for k in range(stages):
                from_u = (u - lags[k]) % turns
                back = p + (u - lags[k] - from_u) // turns

                @pl.when((back >= 0) & (back * turns + from_u < steps))
                def _():
                    finish(back, from_u, k)

    natural = list(range(rows_bits))
    turned = natural[rows_bits // 2 :] + natural[: rows_bits // 2]
    for j in range(rows_bits):
        copies = []
        for h, order in enumerate((natural, turned)):
            copies.append(
                pltpu.make_async_remote_copy(
                    src_ref=col.at[j, h],
                    dst_ref=colr.at[j, h],
                    send_sem=cssem.at[j, h],
                    recv_sem=crsem.at[j, h],
                    device_id=row_partner[order[j]],
                    device_id_type=MESH,
                )
            )
            copies[-1].start()
        for h in range(2):
            copies[h].wait()
            col[j + 1, h] = col[j, h] + colr[j, h]
    clip = jnp.minimum(1.0, 0.5 / jnp.sqrt(sq[last, 0:1, 0:1] / (D * FF) + 1e-06))
    half = col.shape[-1]
    for h in range(2):
        both = col[stages, h]
        scale = jnp.sqrt(both[0:1] / RANK + 1e-06) / jnp.sqrt(both[1:2] / RANK + 1e-06)
        fac[:, h * half : (h + 1) * half] = clip * scale

    @pl.loop(0, steps // turns)
    def _(p):
        for lane in lanes:
            for k in range(stages):
                exchange(p, lane, k).wait_send()


def shards(rows, cols, grad, projection, moment1, moment2):
    depth, span = grad.shape
    rows_bits, cols_bits = rows.bit_length() - 1, cols.bit_length() - 1
    width, turns = 512, 2
    steps = span // width
    own = RANK // rows
    natural = tuple(range(rows_bits))
    orders = (natural, natural[1::-1] + natural[2:], natural[2:] + natural[:2])
    plan = (((0, 0, 128), (1, 128, 128), (2, 256, 256)), ((0, 0, 256), (1, 256, 256)))
    ahead = 2
    lags = tuple(ahead + 2 * k for k in range(rows_bits))
    cfg = (rows_bits, cols_bits, steps, width, orders, plan, lags, ahead)
    pairs = steps // turns
    most = max(wide for turn in plan for _, _, wide in turn)
    last = rows_bits + cols_bits
    f32 = jnp.float32
    vmem = pl.BlockSpec(memory_space=pltpu.VMEM)
    hbm = pl.BlockSpec(memory_space=pl.ANY)
    dma = pltpu.SemaphoreType.DMA
    moment1_new, moment2_new, factor = pl.pallas_call(
        functools.partial(kernel, cfg),
        out_shape=(
            jax.ShapeDtypeStruct((own, span), f32),
            jax.ShapeDtypeStruct((own, span), f32),
            jax.ShapeDtypeStruct((1, span), f32),
        ),
        in_specs=[hbm, hbm, vmem, vmem],
        out_specs=[vmem, vmem, vmem],
        scratch_shapes=[
            pltpu.VMEM((steps, depth, width), f32),
            pltpu.VMEM((len(orders), RANK, depth), f32),
            pltpu.VMEM((last + 1, 8, most), f32),
            pltpu.VMEM((last, 8, most), f32),
            pltpu.VMEM((rows_bits + 1, 2, 2, span // 2), f32),
            pltpu.VMEM((rows_bits, 2, 2, span // 2), f32),
        ]
        + [
            pltpu.VMEM((pairs, RANK >> k, wide), f32)
            for turn in plan
            for _, _, wide in turn
            for k in range(rows_bits + 1)
        ]
        + [
            dma((steps,)),
            dma((len(orders), rows)),
            dma((sum(map(len, plan)), pairs, rows_bits)),
            dma((sum(map(len, plan)), pairs, rows_bits)),
            dma((last,)),
            dma((last,)),
            dma((rows_bits, 2)),
            dma((rows_bits, 2)),
        ],
        compiler_params=pltpu.CompilerParams(
            collective_id=0, has_side_effects=True, vmem_limit_bytes=67000000
        ),
        name="project_reduce",
    )(grad, projection, moment1, moment2)
    return (grad * factor, moment1_new, moment2_new)


def solution(mesh):
    rows, cols = mesh.shape["rows"], mesh.shape["cols"]
    return jax.shard_map(
        functools.partial(shards, rows, cols),
        mesh=mesh,
        in_specs=(P("rows", "cols"), P(None, "rows"), P("rows", "cols"), P("rows", "cols")),
        out_specs=(P("rows", "cols"), P("rows", "cols"), P("rows", "cols")),
        check_vma=False,
    )
```

time: 208 us -> 183 us (0.88)
  Pallas kernels: 194 us -> 169 us
    pallas_call x1, Pallas kernels: 194 us -> 169 us  [shards(): pl.pallas_call(functools.partial(kernel, cfg), out_shape=(jax.ShapeDtypeS...]
where the time goes in v2:
time: 183 us
  Pallas kernels  169 us (92%)
  other arithmetic  11.5 us (6%)
  local copies, waits for them, and re-layouts  1.95 us (1%)
    pallas_call x1, Pallas kernels, shards(): pl.pallas_call(functools.partial(kernel, cfg), out_shape=(jax.ShapeDtypeS...  169 us
    mul x1, other arithmetic, shards(): return (grad * factor, moment1_new, moment2_new)  11.5 us

profile of v2, /device:TPU:0, one launch (start us, length us, event | category | flops | bytes accessed | tf_op | source)
XLA Modules:
  0.0 183.1 jit_solution(16890039336827218393)
XLA Ops:
  0.6 169.0 %project_reduce.1 = (f32[32,8192]{1,0:T(8,128)}, f32[32,8192]{1,0:T(8,128)}, f32[1,8192]{1,0:T(1,128)}) custom-call(f32[384,8192]{1,0:T(8,128)} %grad.1, f32[512,384]{1,0:T(8,128)} %projection.1, f32[32,8192]{1,0:T(8,128)} %m1.1, f32[32,8192]{1,0:T(8,128)} %m2.1), custom_call_target="tpu_custom_call" | custom-call | tf_op jit(solution)/shard_map/project_reduce/pallas_call | solution.py:231
  169.6 0.0 copy-start.1
  169.6 0.0 copy-start
  169.7 11.5 %broadcast_multiply_fusion = f32[384,8192]{1,0:T(8,128)} fusion(f32[384,8192]{1,0:T(8,128)} %grad.1, f32[8192]{0:T(1024)} %bitcast.1), kind=kLoop, calls=%fused_computation | loop fusion | flops 3145728 | bytes 25198592 | tf_op jit(solution)/shard_map/mul | solution.py:269
  181.1 0.0 copy-done.1
  181.1 1.0 copy.9
  182.1 0.0 copy-done
  182.1 1.0 copy.10
Async XLA Ops:
  169.6 11.5 %copy-start.1 = (f32[32,8192]{1,0:T(8,128)S(1)}, f32[32,8192]{1,0:T(8,128)}, u32[]{:S(2)}) copy-start(f32[32,8192]{1,0:T(8,128)} %get-tuple-element.13) | copy-start | bytes 3145732
  169.6 12.4 %copy-start = (f32[32,8192]{1,0:T(8,128)S(1)}, f32[32,8192]{1,0:T(8,128)}, u32[]{:S(2)}) copy-start(f32[32,8192]{1,0:T(8,128)} %get-tuple-element.14) | copy-start | bytes 3145732
